TPU v7x, 32 devices: a whole 2x2x4 slice. The times are simulated.
32 devices in a mesh: grp: 2 (over y), sv: 4 (over z), tv: 4 (over x, core).
Axes of the slice: x: 2, y: 2, z: 4, core: 2. Of those that a mesh axis runs over, the one named last changes fastest.
Arguments:
- student_states: bfloat16 [512, 1792], P('grp', 'tv'), parts along dimension 0, may hold values from -60 to 60
- teacher_states: bfloat16 [512, 2304], P('grp', 'tv'), parts along dimension 0, may hold values from -60 to 60
- student_queries: bfloat16 [512, 256], P('grp', 'tv'), parts along dimension 0, may hold values from -60 to 60
- teacher_keys: bfloat16 [512, 256], P('grp', 'tv'), parts along dimension 0, may hold values from -6 to 6
- student_targets: int32 [512], P('grp'), parts along dimension 0, may hold values from 0 to 8191
- teacher_targets: int32 [512], P('grp'), parts along dimension 0, may hold values from 0 to 8191
- student_lengths: int32 [4], P('grp'), parts along dimension 0, may hold values from 64 to 128
- teacher_lengths: int32 [4], P('grp'), parts along dimension 0, may hold values from 64 to 128
- to_teacher: bfloat16 [1792, 2304], P('tv', 'sv'), may hold values from -0.125 to 0.125
- to_student: bfloat16 [2304, 1792], P('tv', 'sv'), may hold values from -0.125 to 0.125
- student_head: bfloat16 [1792, 8192], P(None, ('sv', 'tv')), may hold values from -0.125 to 0.125
- teacher_head: bfloat16 [2304, 8192], P(None, ('sv', 'tv')), may hold values from -0.125 to 0.125
Outputs:
- student_loss: float32 [512], P('grp'), parts along dimension 0
- teacher_loss: float32 [512], P('grp'), parts along dimension 0
- student_grad: bfloat16 [512, 8192], P('grp', ('sv', 'tv')), parts along dimension 0
- teacher_grad: bfloat16 [512, 8192], P('grp', ('sv', 'tv')), parts along dimension 0
There are 2 independent parts, one for each index of `grp`. A program takes and returns all parts, laid end to end along the dimension named above; an argument that names none is the same for every part. Nothing has to cross between parts.
All inputs are finite; a program needn't handle non-finite values.
Results may differ from a plain program's by a relative error of at most 0.0086.
Values may be sent and summed in bfloat16 or wider, within the bound.
No kernel may reach another device: no remote copies, remote signals or barrier semaphores. Data moves between devices by JAX's collectives and lax.ppermute only.
A program may use at most 64 MiB of HBM per device.

v0:
```python
import jax
import jax.numpy as jnp
from jax import lax
from jax.sharding import PartitionSpec as P

DK = 256
floor_value = -1e30


def combined_all(part, axis, combine):
    gathered = jax.tree.map(lambda a: lax.all_gather(a, axis), part)

    def take(source):
        return jax.tree.map(lambda a: lax.dynamic_index_in_dim(a, source, 0, False), gathered)

    return lax.fori_loop(
        1, lax.axis_size(axis), lambda source, state: combine(state, take(source)), take(0)
    )


def align_block(student_queries, teacher_keys, teacher_states, teacher_lengths):
    sequences = teacher_lengths.shape[0]
    query_cols = student_queries.shape[1]
    queries = student_queries.reshape(sequences, -1, query_cols)
    keyset = teacher_keys.reshape(sequences, -1, query_cols)
    partial_scores = jnp.einsum("sid,sjd->sij", queries, keyset, preferred_element_type=jnp.float32)
    scores = lax.psum(partial_scores, "tv") * DK ** (-0.5)
    positions = lax.broadcasted_iota(jnp.int32, scores.shape, 2)
    scores = jnp.where(positions < teacher_lengths[:, None, None], scores, floor_value)
    highest = jnp.max(scores, axis=2, keepdims=True)
    weights = jnp.exp(scores - highest)
    weights = (weights / jnp.sum(weights, axis=2, keepdims=True)).astype(jnp.bfloat16)
    states = teacher_states.reshape(sequences, -1, teacher_states.shape[1])
    aligned = jnp.einsum("sij,sjd->sid", weights, states, preferred_element_type=jnp.float32)
    return aligned.astype(jnp.bfloat16).reshape(-1, teacher_states.shape[1])


def live_rows(row_count, lengths, sequence_length):
    indices = lax.broadcasted_iota(jnp.int32, (row_count,), 0)
    sequence = indices // sequence_length
    position = indices % sequence_length
    owners = lax.broadcasted_iota(jnp.int32, (row_count, lengths.shape[0]), 1)
    length_limit = jnp.sum(jnp.where(sequence[:, None] == owners, lengths[None, :], 0), axis=1)
    return (position < length_limit).astype(jnp.float32)


def local_stats(logits, target_cols, kind_index):
    other_kind = 1 - kind_index
    highest = jnp.max(logits, axis=2)
    scaled = jnp.exp(logits - highest[:, :, None])
    totals = jnp.sum(scaled, axis=2)
    spread = jnp.sum(
        scaled[:, kind_index] * (logits[:, kind_index] - logits[:, other_kind]), axis=1
    )
    column = lax.broadcasted_iota(jnp.int32, logits.shape, 2)
    picked = jnp.sum(jnp.where(column == target_cols[:, None, None], logits, 0.0), axis=2)
    return (highest, totals, spread, picked)


def side_combine(former, latter, kind_index):
    highest = jnp.maximum(former[0], latter[0])
    former_scale = jnp.exp(former[0] - highest)
    latter_scale = jnp.exp(latter[0] - highest)
    totals = former[1] * former_scale + latter[1] * latter_scale
    spread = former[2] * former_scale[:, kind_index] + latter[2] * latter_scale[:, kind_index]
    return (highest, totals, spread, former[3] + latter[3])


def student_combine(former, latter):
    return side_combine(former, latter, 1)


def teacher_combine(former, latter):
    return side_combine(former, latter, 0)


def side_terms(logits, statistics, target_cols):
    highest, totals = (statistics[0], statistics[1])
    log_total = highest + jnp.log(totals)
    chances = jnp.exp(logits - log_total[:, :, None])
    column = lax.broadcasted_iota(jnp.int32, chances[:, 0].shape, 1)
    target_hot = (column == target_cols[:, None]).astype(jnp.float32)
    return (log_total, chances, target_hot)


def student_side(logits, statistics, target_cols, live_mask):
    log_total, chances, target_hot = side_terms(logits, statistics, target_cols)
    totals, spread, picked = (statistics[1], statistics[2], statistics[3])
    diverge = spread / totals[:, 1] - log_total[:, 1] + log_total[:, 0]
    row_loss = live_mask * (
        log_total[:, 0] - picked[:, 0] + log_total[:, 1] - picked[:, 1] + diverge
    )
    gradient = live_mask[:, None] * (2.0 * chances[:, 0] - target_hot - chances[:, 1])
    return (row_loss, gradient.astype(jnp.bfloat16))


def teacher_side(logits, statistics, target_cols, live_mask):
    log_total, chances, target_hot = side_terms(logits, statistics, target_cols)
    totals, spread, picked = (statistics[1], statistics[2], statistics[3])
    diverge = spread / totals[:, 0] - log_total[:, 0] + log_total[:, 1]
    row_loss = live_mask * (diverge + log_total[:, 1] - picked[:, 1])
    gradient = live_mask[:, None] * (2.0 * chances[:, 1] - chances[:, 0] - target_hot)
    return (row_loss, gradient.astype(jnp.bfloat16))


def body(
    student_states,
    teacher_states,
    student_queries,
    teacher_keys,
    student_targets,
    teacher_targets,
    student_lengths,
    teacher_lengths,
    to_teacher,
    to_student,
    student_head,
    teacher_head,
):
    row_total = student_states.shape[0]
    sequence_length = row_total // student_lengths.shape[0]
    sv_index = lax.axis_index("sv")
    tv_index = lax.axis_index("tv")
    tv_count = lax.axis_size("tv")
    vocab_block = sv_index * tv_count + tv_index
    aligned_block = align_block(student_queries, teacher_keys, teacher_states, teacher_lengths)
    full_student = lax.all_gather(student_states, "tv", axis=1, tiled=True)
    full_aligned = lax.all_gather(aligned_block, "tv", axis=1, tiled=True)
    teacher_part = lax.psum(
        jnp.dot(student_states, to_teacher, preferred_element_type=jnp.float32), "tv"
    )
    student_part = lax.psum(
        jnp.dot(aligned_block, to_student, preferred_element_type=jnp.float32), "tv"
    )
    into_teacher = lax.all_gather(teacher_part.astype(jnp.bfloat16), "sv", axis=1, tiled=True)
    into_student = lax.all_gather(student_part.astype(jnp.bfloat16), "sv", axis=1, tiled=True)
    student_logits = jnp.stack(
        [
            jnp.dot(full_student, student_head, preferred_element_type=jnp.float32),
            jnp.dot(into_student, student_head, preferred_element_type=jnp.float32),
        ],
        axis=1,
    )
    student_cols = student_targets - vocab_block * student_head.shape[1]
    student_stats = local_stats(student_logits, student_cols, 1)
    teacher_logits = jnp.stack(
        [
            jnp.dot(full_aligned, teacher_head, preferred_element_type=jnp.float32),
            jnp.dot(into_teacher, teacher_head, preferred_element_type=jnp.float32),
        ],
        axis=1,
    )
    teacher_cols = teacher_targets - vocab_block * teacher_head.shape[1]
    teacher_stats = local_stats(teacher_logits, teacher_cols, 0)
    student_stats = combined_all(student_stats, ("sv", "tv"), student_combine)
    teacher_stats = combined_all(teacher_stats, ("sv", "tv"), teacher_combine)
    every_live = live_rows(row_total, student_lengths, sequence_length)
    student_loss, student_grad = student_side(
        student_logits, student_stats, student_cols, every_live
    )
    teacher_loss, teacher_grad = teacher_side(
        teacher_logits, teacher_stats, teacher_cols, every_live
    )
    return (student_loss, teacher_loss, student_grad, teacher_grad)


def solution(mesh):
    in_specs = (
        P("grp", "tv"),
        P("grp", "tv"),
        P("grp", "tv"),
        P("grp", "tv"),
        P("grp"),
        P("grp"),
        P("grp"),
        P("grp"),
        P("tv", "sv"),
        P("tv", "sv"),
        P(None, ("sv", "tv")),
        P(None, ("sv", "tv")),
    )
    out_specs = (P("grp"), P("grp"), P("grp", ("sv", "tv")), P("grp", ("sv", "tv")))
    return jax.shard_map(body, mesh=mesh, in_specs=in_specs, out_specs=out_specs, check_vma=False)
```

profile of v0, /device:TPU:0, one launch (start us, length us, event | category | flops | bytes accessed | tf_op | source)
XLA Modules:
  0.0 294.7 jit_solution(5090712872728876629)
XLA Ops:
  7.3 1.8 fusion.30
  9.2 12.4 %all_gather.60 = bf16[256,1792]{0,1:T(8,128)(2,1)} all-gather(bf16[256,448]{0,1:T(8,128)(2,1)} %param.16), channel_id=1, replica_groups=mesh['grp'=2,'sv'=4,'tv'=4] {'tv'}, dimensions={1}, use_global_device_ids=true | all-gather | bytes 1146880 | tf_op jit(solution)/shard_map/all_gather | solution.py:127
  21.6 1.3 fusion.60
  23.0 22.0 %all-reduce.4.cloned.1.call-done = f32[2,128,128]{2,1,0:T(8,128)} async-done(((f32[2,128,128]{2,1,0:T(8,128)}), f32[2,128,128]{2,1,0:T(8,128)}) %all-reduce.4.cloned.1.call-update) | async-done | bytes 131088 | tf_op jit(solution)/shard_map/psum | solution.py:27
  45.1 1.2 fusion.56
  46.3 2.4 fusion.5
  48.7 1.5 fusion.48
  50.1 26.0 %all-reduce.5 = (bf16[256,448]{0,1:T(8,128)(2,1)}, bf16[256,576]{0,1:T(8,128)(2,1)}) all-reduce(f32[256,448]{0,1:T(8,128)S(1)} %fusion.48, f32[256,576]{0,1:T(8,128)S(1)} %fusion.60), channel_id=1, replica_groups=mesh['grp'=2,'sv'=4,'tv'=4] {'tv'}, use_global_device_ids=true, to_apply=%region_4.5 | all-reduce | flops 262144 | bytes 1572864 | tf_op jit(solution)/shard_map/psum | solution.py:132
  76.2 0.6 fusion.47
  76.8 2.6 fusion.57
  79.4 0.8 copy.53
  80.2 33.6 %all_gather.61 = bf16[256,1792]{0,1:T(8,128)(2,1)S(1)} all-gather(bf16[256,448]{0,1:T(8,128)(2,1)S(1)} %copy-done.6), channel_id=1, replica_groups=mesh['grp'=2,'sv'=4,'tv'=4] {'sv'}, dimensions={1}, use_global_device_ids=true | all-gather | bytes 1146880 | tf_op jit(solution)/shard_map/all_gather | solution.py:136
  113.8 0.7 fusion.58
  115.3 20.8 %all-gather.8 = f32[16,1,256]{2,1,0:T(1,128)S(1)} all-gather(f32[1,1,256]{2,1,0:T(1,128)S(1)} %bitcast.187), channel_id=4, replica_groups=mesh['grp'=2,'sv'=4,'tv'=4] {'sv','tv'}, dimensions={0}, use_global_device_ids=true | all-gather | bytes 17408 | tf_op jit(solution)/shard_map/all_gather | solution.py:11
  136.1 17.5 %all-gather = f32[4096,2]{0,1:T(2,128)S(1)} all-gather(f32[256,2]{0,1:T(2,128)S(1)} %get-tuple-element.461), channel_id=2, replica_groups=mesh['grp'=2,'sv'=4,'tv'=4] {'sv','tv'}, dimensions={0}, use_global_device_ids=true | all-gather | bytes 34816 | tf_op jit(solution)/shard_map/all_gather | solution.py:11
  153.6 18.9 %all-gather.1 = f32[4096,2]{0,1:T(2,128)S(1)} all-gather(f32[256,2]{0,1:T(2,128)S(1)} %get-tuple-element.510), channel_id=3, replica_groups=mesh['grp'=2,'sv'=4,'tv'=4] {'sv','tv'}, dimensions={0}, use_global_device_ids=true | all-gather | bytes 34816 | tf_op jit(solution)/shard_map/all_gather | solution.py:11
  172.4 17.5 %all-gather.3 = f32[4096,2]{0,1:T(2,128)S(1)} all-gather(f32[256,2]{0,1:T(2,128)S(1)} %get-tuple-element.460), channel_id=5, replica_groups=mesh['grp'=2,'sv'=4,'tv'=4] {'sv','tv'}, dimensions={0}, use_global_device_ids=true | all-gather | bytes 34816 | tf_op jit(solution)/shard_map/all_gather | solution.py:11
  189.9 1.6 while.42
  191.5 0.6 slice.101
  192.1 0.6 fusion.55
  192.7 0.6 fusion.54
  193.3 2.9 fusion.61
  196.2 9.7 %all-gather.13.cloned.1.call-done = bf16[256,2304]{0,1:T(8,128)(2,1)} async-done(((bf16[256,576]{0,1:T(8,128)(2,1)}), bf16[256,2304]{0,1:T(8,128)(2,1)}) %all-gather.13.cloned.1.call-update) | async-done | bytes 1179664 | tf_op jit(solution)/shard_map/all_gather | solution.py:128
  205.9 2.1 fusion.59
  208.4 20.5 %all-gather.4 = f32[4096,2]{0,1:T(2,128)S(1)} all-gather(f32[256,2]{0,1:T(2,128)S(1)} %get-tuple-element.459), channel_id=6, replica_groups=mesh['grp'=2,'sv'=4,'tv'=4] {'sv','tv'}, dimensions={0}, use_global_device_ids=true | all-gather | bytes 34816 | tf_op jit(solution)/shard_map/all_gather | solution.py:11
  229.4 17.4 %all-gather.9 = f32[16,1,256]{2,1,0:T(1,128)S(1)} all-gather(f32[1,1,256]{2,1,0:T(1,128)S(1)} %bitcast.188), channel_id=8, replica_groups=mesh['grp'=2,'sv'=4,'tv'=4] {'sv','tv'}, dimensions={0}, use_global_device_ids=true | all-gather | bytes 17408 | tf_op jit(solution)/shard_map/all_gather | solution.py:11
  246.8 18.8 %all-gather.5 = f32[4096,2]{0,1:T(2,128)S(1)} all-gather(f32[256,2]{0,1:T(2,128)S(1)} %get-tuple-element.508), channel_id=7, replica_groups=mesh['grp'=2,'sv'=4,'tv'=4] {'sv','tv'}, dimensions={0}, use_global_device_ids=true | all-gather | bytes 34816 | tf_op jit(solution)/shard_map/all_gather | solution.py:11
  265.7 17.5 %all-gather.7 = f32[4096,2]{0,1:T(2,128)S(1)} all-gather(f32[256,2]{0,1:T(2,128)S(1)} %get-tuple-element.458), channel_id=9, replica_groups=mesh['grp'=2,'sv'=4,'tv'=4] {'sv','tv'}, dimensions={0}, use_global_device_ids=true | all-gather | bytes 34816 | tf_op jit(solution)/shard_map/all_gather | solution.py:11
  283.2 1.6 while.43
  284.8 1.5 subtract_exponential_fusion.2
  286.4 1.1 fusion.11
  287.6 0.6 fusion.37
  (220 shorter events, 3.9 us)
Async XLA Ops:
  7.2 186.1 %copy-start = (bf16[2304,512]{1,0:T(8,128)(2,1)S(1)}, bf16[2304,512]{1,0:T(8,128)(2,1)}, u32[]{:S(2)}) copy-start(bf16[2304,512]{1,0:T(8,128)(2,1)} %param.27) | copy-start | bytes 7077892
  7.2 14.4 %copy-start.5 = (bf16[448,576]{1,0:T(8,128)(2,1)S(1)}, bf16[448,576]{1,0:T(8,128)(2,1)}, u32[]{:S(2)}) copy-start(bf16[448,576]{1,0:T(8,128)(2,1)} %param.24) | copy-start | bytes 1548292
  7.2 15.7 %copy-start.15 = (s32[256]{0:T(256)S(1)}, s32[256]{0:T(256)}, u32[]{:S(2)}) copy-start(s32[256]{0:T(256)} %param.21) | copy-start | bytes 3076
  7.2 15.7 %copy-start.16 = (s32[256]{0:T(256)S(1)}, s32[256]{0:T(256)}, u32[]{:S(2)}) copy-start(s32[256]{0:T(256)} %param.20) | copy-start | bytes 3076
  7.2 15.7 %copy-start.17 = (s32[2]{0:T(128)S(1)}, s32[2]{0:T(128)}, u32[]{:S(2)}) copy-start(s32[2]{0:T(128)} %param.22) | copy-start | bytes 28
  7.2 37.9 %copy-start.18 = (s32[2]{0:T(128)S(1)}, s32[2]{0:T(128)}, u32[]{:S(2)}) copy-start(s32[2]{0:T(128)} %param.23) | copy-start | bytes 28
  7.2 37.9 %all-reduce.4.cloned.1.call-start = ((), (), s32[]{:S(2)}) async-start(), calls=%async_computation | async-start | bytes 262144 | tf_op jit(solution)/shard_map/psum | solution.py:27
  9.1 184.2 %all-gather.15.cloned.1.call-start = ((), (), s32[]{:S(2)}) async-start(), calls=%async_computation.2 | async-start | bytes 1474560 | tf_op jit(solution)/shard_map/all_gather | solution.py:135
  23.0 53.2 %copy-start.7 = (s32[256]{0:T(256)}, s32[256]{0:T(256)S(1)}, u32[]{:S(2)}) copy-start(s32[256]{0:T(256)S(1)} %fusion.35) | copy-start | bytes 3076
  76.2 3.2 %copy-start.4 = (bf16[2,72,8,128]{3,2,1,0:T(8,128)(2,1)S(1)}, bf16[2,72,8,128]{3,2,1,0:T(8,128)(2,1)}, u32[]{:S(2)}) copy-start(bf16[2,72,8,128]{3,2,1,0:T(8,128)(2,1)} %fusion.5) | copy-start | bytes 884740
  76.2 129.7 %all-gather.13.cloned.1.call-start = ((), (), s32[]{:S(2)}) async-start(), calls=%async_computation.1 | async-start | bytes 1474560 | tf_op jit(solution)/shard_map/all_gather | solution.py:128
  76.8 3.4 %copy-start.6 = (bf16[256,448]{0,1:T(8,128)(2,1)S(1)}, bf16[256,448]{0,1:T(8,128)(2,1)}, u32[]{:S(2)}) copy-start(bf16[256,448]{0,1:T(8,128)(2,1)} %get-tuple-element.498) | copy-start | bytes 688132
  76.8 37.0 %copy-start.3 = (bf16[1792,512]{1,0:T(8,128)(2,1)S(1)}, bf16[1792,512]{1,0:T(8,128)(2,1)}, u32[]{:S(2)}) copy-start(bf16[1792,512]{1,0:T(8,128)(2,1)} %param.26) | copy-start | bytes 5505028
  205.9 2.1 copy-start.1
  208.0 21.3 %copy-start.2 = (f32[256,512]{1,0:T(8,128)}, f32[256,512]{1,0:T(8,128)S(1)}, u32[]{:S(2)}) copy-start(f32[256,512]{1,0:T(8,128)S(1)} %fusion.59) | copy-start | bytes 1572868
  284.8 1.6 copy-start.9
  286.4 1.2 copy-start.8
  286.4 1.2 copy-start.10
  286.4 1.2 copy-start.11
  286.4 1.2 copy-start.12
  286.4 1.2 copy-start.13
  286.4 1.2 copy-start.14
Sparse Core Ops, SparseCore 0:
  11.0 34.0 all-reduce.3
  76.3 43.0 all-gather.14
  190.0 15.8 all-gather.12
where the time goes:
time: 295 us
  blocking collectives  221 us (75%)
  waiting for transfers between devices  31.8 us (11%)
  matrix products  15.3 us (5%)
  between operations  14.1 us (5%)
  other arithmetic  8 us (3%)
  local copies, waits for them, and re-layouts  3.24 us (1%)
    all_gather x8, blocking collectives, combined_all(): gathered = jax.tree.map(lambda a: lax.all_gather(a, axis), part)  149 us
    all_gather x1, blocking collectives, body(): lax.all_gather(student_part.astype(jnp.bfloat16), 'sv', axis=1, tiled=True)  33.6 us
    psum x1, blocking collectives, body(): lax.psum(jnp.dot(aligned_block, to_student, preferred_element_type=jnp.fl...  26 us
    psum x1, waiting for transfers between devices, align_block(): scores = lax.psum(partial_scores, 'tv') * DK ** (-0.5)  22 us
    all_gather x1, blocking collectives, body(): full_student = lax.all_gather(student_states, 'tv', axis=1, tiled=True)  12.4 us
    all_gather x1, waiting for transfers between devices, body(): full_aligned = lax.all_gather(aligned_block, 'tv', axis=1, tiled=True)  9.69 us
  transfers between devices with their start and end apart: 3, of which 2 were waited for; matrix products, arithmetic and copies ran while one was open for 4% of the time, Pallas kernels for 0%

commit v1 on v0

--- a/solution.py
+++ b/solution.py
@@ -125,7 +125,12 @@
     vocab_block = sv_index * tv_count + tv_index
     aligned_block = align_block(student_queries, teacher_keys, teacher_states, teacher_lengths)
     full_student = lax.all_gather(student_states, "tv", axis=1, tiled=True)
-    full_aligned = lax.all_gather(aligned_block, "tv", axis=1, tiled=True)
+    ring = [aligned_block]
+    for hop in range(3):
+        ring.append(lax.ppermute(ring[-1], "tv", [(dev, (dev + 1) % 4) for dev in range(4)]))
+    full_aligned = jnp.roll(
+        jnp.concatenate(ring[::-1], axis=1), (lax.axis_index("tv") + 1) * ring[0].shape[1], axis=1
+    )
     teacher_part = lax.psum(
         jnp.dot(student_states, to_teacher, preferred_element_type=jnp.float32), "tv"
     )

time: 295 us -> 285 us (0.966)
  blocking collectives: 221 us -> 208 us
  local copies, waits for them, and re-layouts: 3.24 us -> 8.24 us
  waiting for transfers between devices: 31.8 us -> 27.1 us
    all_gather x1, blocking collectives: 33.6 us -> 21.2 us  [body(): lax.all_gather(student_part.astype(jnp.bfloat16), 'sv', axis=1, tiled=True)]
    all_gather x1 -> x0, waiting for transfers between devices: 9.69 us -> none  [body(): full_aligned = lax.all_gather(aligned_block, 'tv', axis=1, tiled=True)]
    ppermute x0 -> x3, waiting for transfers between devices: none -> 9.16 us  [body(): lax.ppermute(ring[-1], 'tv', [(dev, (dev + 1) % 4) for dev in range(4)])]
    unnamed x40 -> x43, local copies, waits for them, and re-layouts: 0.09 us -> 5.05 us
    psum x1, waiting for transfers between devices: 22 us -> 17.9 us  [align_block(): scores = lax.psum(partial_scores, 'tv') * DK ** (-0.5)]
  transfers between devices with their start and end apart: 3 -> 5, of which waited for: 2 -> 3; matrix products, arithmetic and copies ran while one was open for 4% -> 6% of each run, Pallas kernels for 0% -> 0%
where the time goes in v1:
time: 285 us; the launch traced here: 284 us
  blocking collectives  208 us (73%)
  waiting for transfers between devices  27.1 us (10%)
  matrix products  16.3 us (6%)
  between operations  14.4 us (5%)
  other arithmetic  8.67 us (3%)
  local copies, waits for them, and re-layouts  8.24 us (3%)
    all_gather x8, blocking collectives, combined_all(): gathered = jax.tree.map(lambda a: lax.all_gather(a, axis), part)  147 us
    psum x1, blocking collectives, body(): lax.psum(jnp.dot(aligned_block, to_student, preferred_element_type=jnp.fl...  27.4 us
    all_gather x1, blocking collectives, body(): lax.all_gather(student_part.astype(jnp.bfloat16), 'sv', axis=1, tiled=True)  21.2 us
    psum x1, waiting for transfers between devices, align_block(): scores = lax.psum(partial_scores, 'tv') * DK ** (-0.5)  17.9 us
    all_gather x1, blocking collectives, body(): full_student = lax.all_gather(student_states, 'tv', axis=1, tiled=True)  12.4 us
    ppermute x3, waiting for transfers between devices, body(): lax.ppermute(ring[-1], 'tv', [(dev, (dev + 1) % 4) for dev in range(4)])  9.16 us
  transfers between devices with their start and end apart: 5, of which 3 were waited for; matrix products, arithmetic and copies ran while one was open for 6% of the time, Pallas kernels for 0%

profile of v1, /device:TPU:0, one launch (start us, length us, event | category | flops | bytes accessed | tf_op | source)
XLA Modules:
  0.0 284.3 jit_solution(8702338200053395282)
XLA Ops:
  7.3 1.8 fusion.32
  9.2 12.4 %all_gather.57 = bf16[256,1792]{0,1:T(8,128)(2,1)} all-gather(bf16[256,448]{0,1:T(8,128)(2,1)} %param.16), channel_id=1, replica_groups=mesh['grp'=2,'sv'=4,'tv'=4] {'tv'}, dimensions={1}, use_global_device_ids=true | all-gather | bytes 1146880 | tf_op jit(solution)/shard_map/all_gather | solution.py:127
  21.5 2.4 fusion.62
  24.1 2.4 fusion.60
  27.1 17.9 %all-reduce.4.cloned.1.call-done = f32[2,128,128]{2,1,0:T(8,128)} async-done(((f32[2,128,128]{2,1,0:T(8,128)}), f32[2,128,128]{2,1,0:T(8,128)}) %all-reduce.4.cloned.1.call-update) | async-done | bytes 131088 | tf_op jit(solution)/shard_map/psum | solution.py:27
  45.1 1.2 fusion.59
  46.2 1.5 fusion.7
  48.7 2.2 fusion.51
  50.9 27.4 %all-reduce.5 = (bf16[256,448]{0,1:T(8,128)(2,1)S(1)}, bf16[256,576]{0,1:T(8,128)(2,1)}) all-reduce(f32[256,448]{0,1:T(8,128)} %fusion.51, f32[256,576]{0,1:T(8,128)} %fusion.62), channel_id=1, replica_groups=mesh['grp'=2,'sv'=4,'tv'=4] {'tv'}, use_global_device_ids=true, to_apply=%region_4.5 | all-reduce | flops 262144 | bytes 1572864 | tf_op jit(solution)/shard_map/psum | solution.py:137
  78.2 21.2 %all_gather.58 = bf16[256,1792]{0,1:T(8,128)(2,1)S(1)} all-gather(bf16[256,448]{0,1:T(8,128)(2,1)S(1)} %get-tuple-element.498), channel_id=1, replica_groups=mesh['grp'=2,'sv'=4,'tv'=4] {'sv'}, dimensions={1}, use_global_device_ids=true | all-gather | bytes 1146880 | tf_op jit(solution)/shard_map/all_gather | solution.py:141
  99.4 2.1 fusion.61
  102.4 20.1 %all-gather.8 = f32[16,1,256]{2,1,0:T(1,128)S(1)} all-gather(f32[1,1,256]{2,1,0:T(1,128)S(1)} %bitcast.189), channel_id=4, replica_groups=mesh['grp'=2,'sv'=4,'tv'=4] {'sv','tv'}, dimensions={0}, use_global_device_ids=true | all-gather | bytes 17408 | tf_op jit(solution)/shard_map/all_gather | solution.py:11
  122.5 17.8 %all-gather = f32[4096,2]{0,1:T(2,128)S(1)} all-gather(f32[256,2]{0,1:T(2,128)S(1)} %get-tuple-element.461), channel_id=2, replica_groups=mesh['grp'=2,'sv'=4,'tv'=4] {'sv','tv'}, dimensions={0}, use_global_device_ids=true | all-gather | bytes 34816 | tf_op jit(solution)/shard_map/all_gather | solution.py:11
  140.4 18.8 %all-gather.1 = f32[4096,2]{0,1:T(2,128)S(1)} all-gather(f32[256,2]{0,1:T(2,128)S(1)} %get-tuple-element.510), channel_id=3, replica_groups=mesh['grp'=2,'sv'=4,'tv'=4] {'sv','tv'}, dimensions={0}, use_global_device_ids=true | all-gather | bytes 34816 | tf_op jit(solution)/shard_map/all_gather | solution.py:11
  159.1 17.6 %all-gather.3 = f32[4096,2]{0,1:T(2,128)S(1)} all-gather(f32[256,2]{0,1:T(2,128)S(1)} %get-tuple-element.460), channel_id=5, replica_groups=mesh['grp'=2,'sv'=4,'tv'=4] {'sv','tv'}, dimensions={0}, use_global_device_ids=true | all-gather | bytes 34816 | tf_op jit(solution)/shard_map/all_gather | solution.py:11
  177.1 1.6 while.42
  178.7 4.5 %collective-permute-done.1 = bf16[256,576]{0,1:T(8,128)(2,1)} collective-permute-done((bf16[256,576]{0,1:T(8,128)(2,1)}, bf16[256,576]{0,1:T(8,128)(2,1)}, u32[]{:S(2)}, u32[]{:S(2)}) %collective-permute-start.1) | collective-permute-done | bytes 294944 | tf_op jit(solution)/shard_map/ppermute | solution.py:130
  184.9 4.6 %collective-permute-done.2 = bf16[256,576]{0,1:T(8,128)(2,1)S(1)} collective-permute-done((bf16[256,576]{0,1:T(8,128)(2,1)}, bf16[256,576]{0,1:T(8,128)(2,1)S(1)}, u32[]{:S(2)}, u32[]{:S(2)}) %collective-permute-start.2) | collective-permute-done | bytes 294944 | tf_op jit(solution)/shard_map/ppermute | solution.py:130
  189.6 1.0 constant_dynamic-update-slice_fusion.6
  190.6 1.0 constant_dynamic-update-slice_fusion.5
  191.5 1.0 constant_dynamic-update-slice_fusion.4
  192.6 1.0 constant_dynamic-update-slice_fusion.2
  193.6 1.0 constant_dynamic-update-slice_fusion.1
  194.6 1.6 fusion.5
  196.3 2.1 fusion.63
  198.8 18.7 %all-gather.4 = f32[4096,2]{0,1:T(2,128)S(1)} all-gather(f32[256,2]{0,1:T(2,128)S(1)} %get-tuple-element.459), channel_id=6, replica_groups=mesh['grp'=2,'sv'=4,'tv'=4] {'sv','tv'}, dimensions={0}, use_global_device_ids=true | all-gather | bytes 34816 | tf_op jit(solution)/shard_map/all_gather | solution.py:11
  218.0 17.5 %all-gather.9 = f32[16,1,256]{2,1,0:T(1,128)S(1)} all-gather(f32[1,1,256]{2,1,0:T(1,128)S(1)} %bitcast.190), channel_id=8, replica_groups=mesh['grp'=2,'sv'=4,'tv'=4] {'sv','tv'}, dimensions={0}, use_global_device_ids=true | all-gather | bytes 17408 | tf_op jit(solution)/shard_map/all_gather | solution.py:11
  235.5 18.7 %all-gather.5 = f32[4096,2]{0,1:T(2,128)S(1)} all-gather(f32[256,2]{0,1:T(2,128)S(1)} %get-tuple-element.508), channel_id=7, replica_groups=mesh['grp'=2,'sv'=4,'tv'=4] {'sv','tv'}, dimensions={0}, use_global_device_ids=true | all-gather | bytes 34816 | tf_op jit(solution)/shard_map/all_gather | solution.py:11
  254.3 17.6 %all-gather.7 = f32[4096,2]{0,1:T(2,128)S(1)} all-gather(f32[256,2]{0,1:T(2,128)S(1)} %get-tuple-element.458), channel_id=9, replica_groups=mesh['grp'=2,'sv'=4,'tv'=4] {'sv','tv'}, dimensions={0}, use_global_device_ids=true | all-gather | bytes 34816 | tf_op jit(solution)/shard_map/all_gather | solution.py:11
  271.9 1.5 while.43
  273.5 1.5 subtract_exponential_fusion.2
  275.1 1.8 fusion.13
  (227 shorter events, 7.9 us)
Async XLA Ops:
  7.2 187.4 %copy-start = (bf16[2304,512]{1,0:T(8,128)(2,1)S(1)}, bf16[2304,512]{1,0:T(8,128)(2,1)}, u32[]{:S(2)}) copy-start(bf16[2304,512]{1,0:T(8,128)(2,1)} %param.27) | copy-start | bytes 7077892
  7.2 16.8 %copy-start.12 = (s32[256]{0:T(256)S(1)}, s32[256]{0:T(256)}, u32[]{:S(2)}) copy-start(s32[256]{0:T(256)} %param.21) | copy-start | bytes 3076
  7.2 16.8 %copy-start.13 = (s32[256]{0:T(256)S(1)}, s32[256]{0:T(256)}, u32[]{:S(2)}) copy-start(s32[256]{0:T(256)} %param.20) | copy-start | bytes 3076
  7.2 16.8 %copy-start.14 = (s32[2]{0:T(128)S(1)}, s32[2]{0:T(128)}, u32[]{:S(2)}) copy-start(s32[2]{0:T(128)} %param.22) | copy-start | bytes 28
  7.2 37.9 %all-reduce.4.cloned.1.call-start = ((), (), s32[]{:S(2)}) async-start(), calls=%async_computation | async-start | bytes 262144 | tf_op jit(solution)/shard_map/psum | solution.py:27
  9.1 187.2 %all-gather.12.cloned.1.call-start = ((), (), s32[]{:S(2)}) async-start(), calls=%async_computation.1 | async-start | bytes 1474560 | tf_op jit(solution)/shard_map/all_gather | solution.py:140
  21.5 23.5 %copy-start.16 = (s32[2]{0:T(128)S(1)}, s32[2]{0:T(128)}, u32[]{:S(2)}) copy-start(s32[2]{0:T(128)} %param.23) | copy-start | bytes 28
  21.5 24.7 %copy-start.15 = (bf16[256,576]{0,1:T(8,128)(2,1)S(1)}, bf16[256,576]{0,1:T(8,128)(2,1)}, u32[]{:S(2)}) copy-start(bf16[256,576]{0,1:T(8,128)(2,1)} %param.17) | copy-start | bytes 884740
  24.1 21.0 %copy-start.5 = (s32[256]{0:T(256)}, s32[256]{0:T(256)S(1)}, u32[]{:S(2)}) copy-start(s32[256]{0:T(256)S(1)} %fusion.37) | copy-start | bytes 3076
  47.8 30.4 %copy-start.3 = (bf16[2,72,8,128]{3,2,1,0:T(8,128)(2,1)}, bf16[2,72,8,128]{3,2,1,0:T(8,128)(2,1)S(1)}, u32[]{:S(2)}) copy-start(bf16[2,72,8,128]{3,2,1,0:T(8,128)(2,1)S(1)} %fusion.7) | copy-start | bytes 884740
  50.8 125.9 %collective-permute-start = (bf16[256,576]{0,1:T(8,128)(2,1)}, bf16[256,576]{0,1:T(8,128)(2,1)}, u32[]{:S(2)}, u32[]{:S(2)}) collective-permute-start(bf16[256,576]{0,1:T(8,128)(2,1)} %bitcast.133), channel_id=1, source_target_pairs={{0,1},{1,2},{2,3},{3,0},{4,5},{5,6},{6,7},{7,4},{8,9},{9,10},{10,1... | collective-permute-start | bytes 884744 | tf_op jit(solution)/shard_map/ppermute | solution.py:130
  176.7 6.5 %collective-permute-start.1 = (bf16[256,576]{0,1:T(8,128)(2,1)}, bf16[256,576]{0,1:T(8,128)(2,1)}, u32[]{:S(2)}, u32[]{:S(2)}) collective-permute-start(bf16[256,576]{0,1:T(8,128)(2,1)} %collective-permute-done), channel_id=1, source_target_pairs={{0,1},{1,2},{2,3},{3,0},{4,5},{5,6},{6,7},{7,4},{8,9},{9,10},{10,1... | collective-permute-start | bytes 884744 | tf_op jit(solution)/shard_map/ppermute | solution.py:130
  178.6 15.9 %copy-start.4 = (bf16[2,72,8,128]{3,2,1,0:T(8,128)(2,1)S(1)}, bf16[2,72,8,128]{3,2,1,0:T(8,128)(2,1)}, u32[]{:S(2)}) copy-start(bf16[2,72,8,128]{3,2,1,0:T(8,128)(2,1)} %copy-done.3) | copy-start | bytes 884740
  183.2 6.4 %collective-permute-start.2 = (bf16[256,576]{0,1:T(8,128)(2,1)}, bf16[256,576]{0,1:T(8,128)(2,1)S(1)}, u32[]{:S(2)}, u32[]{:S(2)}) collective-permute-start(bf16[256,576]{0,1:T(8,128)(2,1)} %collective-permute-done.1), channel_id=1, source_target_pairs={{0,1},{1,2},{2,3},{3,0},{4,5},{5,6},{6,7},{7,4},{8,9},{9,10},{10,1... | collective-permute-start | bytes 884744 | tf_op jit(solution)/shard_map/ppermute | solution.py:130
  196.3 2.1 copy-start.1
  198.4 19.6 %copy-start.2 = (f32[256,512]{1,0:T(8,128)}, f32[256,512]{1,0:T(8,128)S(1)}, u32[]{:S(2)}) copy-start(f32[256,512]{1,0:T(8,128)S(1)} %fusion.63) | copy-start | bytes 1572868
  275.0 1.9 copy-start.6
  275.0 1.9 copy-start.7
  275.0 1.8 copy-start.8
  275.0 1.8 copy-start.9
  275.0 1.8 copy-start.10
  275.1 1.8 copy-start.11
Sparse Core Ops, SparseCore 0:
  10.9 34.0 all-reduce.3
  122.7 27.3 all-gather.11
